TPU v7x, 32 devices: a whole 2x2x4 slice. The times are simulated.
32 devices in a mesh: group: 2 (over y), expert: 4 (over z), dp: 4 (over x, core).
Axes of the slice: x: 2, y: 2, z: 4, core: 2. Of those that a mesh axis runs over, the one named last changes fastest.
Arguments:
- tokens: bfloat16 [256, 4096], P(('group', 'expert', 'dp')), parts along dimension 0, may hold values from -6 to 6
- routing: int32 [256, 8], P(('group', 'expert', 'dp')), parts along dimension 0, may hold values from 0 to 127, as said below
- gate_quantized: int32 [256, 8], P(('group', 'expert', 'dp')), parts along dimension 0, may hold values from 1 to 32767
- tenant: int32 [256], P(('group', 'expert', 'dp')), parts along dimension 0, may hold values from 0 to 23
- tenant_page_lookup: int32 [4, 24], replicated, may hold values from 0 to 23, each once within a row
- gate_weight: bfloat16 [4, 4096, 1024], P('expert', None, 'dp'), may hold values from -0.09375 to 0.09375
- up_projection: bfloat16 [4, 4096, 1024], P('expert', None, 'dp'), may hold values from -0.09375 to 0.09375
- down_weight: bfloat16 [4, 1024, 4096], P('expert', None, 'dp'), may hold values from -0.1875 to 0.1875
- adapter_shrink: bfloat16 [4, 24, 16, 4096], P('expert', 'dp'), may hold values from -0.09375 to 0.09375
- adapter_expand: bfloat16 [4, 24, 16, 1024], P('expert', 'dp'), may hold values from -1.5 to 1.5
Outputs:
- mixed_out: bfloat16 [256, 4096], P(('group', 'expert', 'dp')), parts along dimension 0
There are 2 independent parts, one for each index of `group`. A program takes and returns all parts, laid end to end along the dimension named above; an argument that names none is the same for every part. Nothing has to cross between parts.
Inputs may be any that keep to these rules, and one draw needn't show every extreme that they name: `routing`: each row names 8 different experts. Among the 8 tokens of one device no expert is named more than 2 times, and in every draw some expert below 4 is named exactly 2 times by the tokens of every device. `tenant_page_lookup`: row e gives every tenant a different page of expert e's pool.
All inputs are finite; a program needn't handle non-finite values.
Results may differ from a plain program's by a relative error of at most 0.0061.
Values may be sent and summed in bfloat16 or wider, within the bound.
A program may use at most 64 MiB of HBM per device.

v0:
```python
import jax
import jax.numpy as jnp
from jax import lax
from jax.sharding import PartitionSpec as P


def slot_tables(routing, experts, capacity):
    expert_ids = jnp.arange(experts, dtype=jnp.int32)
    matches = routing[:, :, None] == expert_ids[None, None, :]
    assign = jnp.sum(matches.astype(jnp.int32), axis=1)
    slot_rank = jnp.cumsum(assign, axis=0) - assign
    scale_levels = jnp.arange(capacity, dtype=jnp.int32)
    placing = (assign.T[:, None, :] == 1) & (slot_rank.T[:, None, :] == scale_levels[None, :, None])
    return (matches, slot_rank, placing)


def per_device(
    tokens,
    routing,
    gate_quantized,
    tenant,
    tenant_page_lookup,
    gate_weight,
    up_projection,
    down_weight,
    adapter_shrink,
    adapter_expand,
):
    tok_count, model_width = tokens.shape
    experts, tenants = tenant_page_lookup.shape
    capacity = tok_count // 4
    rank_extent = adapter_shrink.shape[2]
    part_width = down_weight.shape[2]
    my_expert = lax.axis_index("expert")
    matches, slot_rank, placing = slot_tables(routing, experts, capacity)
    send_rows = jnp.einsum(
        "ect,td->ecd", placing.astype(jnp.bfloat16), tokens, preferred_element_type=jnp.float32
    ).astype(jnp.bfloat16)
    send_ten = jnp.sum(placing.astype(jnp.int32) * (tenant[None, None, :] + 1), axis=2)
    got_rows, got_ten = (
        lax.all_to_all(send_rows, "expert", split_axis=0, concat_axis=0, tiled=True),
        lax.all_to_all(send_ten, "expert", split_axis=0, concat_axis=0, tiled=True),
    )
    slot_rows, slot_ten = (
        lax.all_gather(got_rows[None], "dp", axis=0, tiled=True),
        lax.all_gather(got_ten[None], "dp", axis=0, tiled=True),
    )
    block_shape = slot_rows.shape[:3]
    slot_count = block_shape[0] * block_shape[1] * block_shape[2]
    slot_input = slot_rows.reshape(slot_count, model_width)
    slot_tenant = slot_ten.reshape(slot_count)
    page_row = lax.dynamic_index_in_dim(tenant_page_lookup, my_expert, 0, keepdims=False)
    tenant_ids = jnp.arange(tenants, dtype=jnp.int32)
    tenant_hot = slot_tenant[:, None] == tenant_ids[None, :] + 1
    slot_page = jnp.sum(jnp.where(tenant_hot, page_row[None, :], 0), axis=1)
    occupied = slot_tenant > 0
    page_pick = ((slot_page[:, None] == tenant_ids[None, :]) & occupied[:, None]).astype(
        jnp.float32
    )
    partial_terms = lax.all_gather(adapter_shrink, "dp", axis=1, tiled=True)
    page_count = partial_terms.shape[1]
    flat_pages = partial_terms.reshape(page_count * rank_extent, model_width)
    products = lax.dot_general(
        slot_input, flat_pages, (((1,), (1,)), ((), ())), preferred_element_type=jnp.float32
    )
    shrink_result = jnp.sum(
        page_pick[:, :, None] * products.reshape(slot_count, page_count, rank_extent), axis=1
    )
    shrink_low = shrink_result.astype(jnp.bfloat16)
    expand_every_page = lax.all_to_all(
        adapter_expand, "dp", split_axis=3, concat_axis=1, tiled=True
    )[0]
    hidden_part = expand_every_page.shape[2]
    expand_matrix = expand_every_page.reshape(tenants * rank_extent, hidden_part)
    spread_rows = (page_pick[:, :, None] * shrink_low.astype(jnp.float32)[:, None, :]).astype(
        jnp.bfloat16
    )
    spread_rows = spread_rows.reshape(slot_count, tenants * rank_extent)
    adapter_update = jnp.dot(spread_rows, expand_matrix, preferred_element_type=jnp.float32)
    gate_act = jnp.dot(slot_input, gate_weight[0], preferred_element_type=jnp.float32)
    up_activation = (
        jnp.dot(slot_input, up_projection[0], preferred_element_type=jnp.float32) + adapter_update
    )
    hidden = (jax.nn.silu(gate_act) * up_activation).astype(jnp.bfloat16)
    weights = down_weight[0]
    expert_out = jnp.dot(
        lax.all_gather(hidden, "dp", axis=1, tiled=True),
        weights,
        preferred_element_type=jnp.float32,
    )
    expert_out = expert_out.astype(jnp.bfloat16).reshape(block_shape + (part_width,))
    home_rows = lax.all_to_all(expert_out, "dp", split_axis=0, concat_axis=3, tiled=True)
    back_rows = lax.all_to_all(home_rows, "expert", split_axis=1, concat_axis=0, tiled=True)
    back_rows = back_rows.reshape(experts * capacity, model_width)
    chosen_rank = jnp.sum(jnp.where(matches, slot_rank[:, None, :], 0), axis=2)
    inside = routing < experts
    flat_index = routing * capacity + chosen_rank
    slot_ids = jnp.arange(experts * capacity, dtype=jnp.int32)
    row_picks = ((flat_index[:, :, None] == slot_ids[None, None, :]) & inside[:, :, None]).astype(
        jnp.bfloat16
    )
    picked = jnp.einsum("tkm,md->tkd", row_picks, back_rows, preferred_element_type=jnp.float32)
    mix_coef = jnp.where(inside, gate_quantized.astype(jnp.float32) / 32768.0, jnp.float32(0.0))
    mixed_out = jnp.sum(mix_coef[:, :, None] * picked, axis=1)
    return mixed_out.astype(jnp.bfloat16)


def solution(mesh):
    return jax.shard_map(
        per_device,
        mesh=mesh,
        in_specs=(
            P(("group", "expert", "dp"), None),
            P(("group", "expert", "dp"), None),
            P(("group", "expert", "dp"), None),
            P(("group", "expert", "dp")),
            P(),
            P("expert", None, "dp"),
            P("expert", None, "dp"),
            P("expert", None, "dp"),
            P("expert", "dp", None, None),
            P("expert", "dp", None, None),
        ),
        out_specs=P(("group", "expert", "dp"), None),
        check_vma=False,
    )
```

profile of v0, /device:TPU:0, one launch (start us, length us, event | category | flops | bytes accessed | tf_op | source)
XLA Modules:
  0.0 94.2 jit_solution(14872100671156031645)
XLA Ops:
  6.5 0.0 copy-start
  6.5 0.0 all-gather.4.cloned.1.call-start
  6.5 0.7 all-gather.4.cloned.1.call-update
  7.3 0.8 convert_reduce_fusion
  8.1 0.2 reduce_window_sum.11
  8.3 0.7 broadcast_add_fusion
  9.0 0.1 select_reduce_fusion.2
  9.1 0.7 copy.39
  9.8 6.3 %all-to-all-start.1 = ((s32[4,1,2]{2,1,0:T(1,128)}), s32[4,1,2]{2,1,0:T(1,128)S(1)}, u32[]{:S(2)}, u32[]{:S(2)}) async-start(s32[4,1,2]{2,1,0:T(1,128)} %copy.39), calls=%async_computation.1 | async-start | bytes 4096 | tf_op jit(solution)/shard_map/all_to_all | solution.py:42
  16.1 1.0 %convolution_convert_fusion = bf16[4,2,4096]{2,0,1:T(4,128)(2,1)S(1)} fusion(bf16[8,4096]{1,0:T(8,128)(2,1)} %param.10, s32[4,8]{1,0:T(4,128)S(1)} %bitcast.58, pred[4,8]{1,0:T(4,128)(4,1)S(1)} %compare_bitcast_fusion), kind=kOutput, calls=%fused_computation.1 | convolution fusion | flops 557184 | bytes 131232 | tf_op jit(solution)/shard_map/ect,td->ecd/dot_general | solution.py:36
  17.1 0.7 copy.38
  17.8 0.0 copy-start.2
  17.8 0.0 copy-start.3
  17.8 3.3 %copy.43 = bf16[1,6,16,1024]{2,1,0,3:T(8,128)(2,1)} copy(bf16[1,6,16,1024]{3,2,1,0:T(8,128)(2,1)} %param.19) | data formatting | bytes 393216 | tf_op args[9]
  21.2 3.5 %reshape.122 = bf16[4,2,12288]{2,1,0:T(2,128)(2,1)} reshape(bf16[1024,1,6,16]{3,2,1,0:T(8,128)(2,1)} %bitcast.51) | data formatting | bytes 393216
  24.7 0.7 dynamic-slice_bitcast_fusion
  25.4 0.0 copy-done.2
  25.4 0.0 copy-done.3
  25.4 0.0 all-to-all-done.1
  25.4 5.1 %all-to-all-start = ((bf16[4,2,4096]{2,1,0:T(2,128)(2,1)}), bf16[4,2,4096]{2,1,0:T(2,128)(2,1)S(1)}, u32[]{:S(2)}, u32[]{:S(2)}) async-start(bf16[4,2,4096]{2,1,0:T(2,128)(2,1)} %copy.38), calls=%async_computation | async-start | bytes 131072 | tf_op jit(solution)/shard_map/all_to_all | solution.py:41
  30.5 5.3 %all-gather.1 = s32[16,1,2]{2,1,0:T(1,128)S(1)} all-gather(s32[4,1,2]{2,1,0:T(1,128)S(1)} %all-to-all-done.1), channel_id=3, replica_groups=mesh['group'=2,'expert'=4,'dp'=4] {'dp'}, dimensions={0}, use_global_device_ids=true | all-gather | bytes 160 | tf_op jit(solution)/shard_map/all_gather | solution.py:46
  35.8 0.5 broadcast.74
  36.3 0.6 reduce.3
  36.9 0.1 eq.93
  37.0 0.1 select_reduce_fusion.1
  37.1 0.0 all-to-all-done
  37.1 3.4 %all-to-all-start.2 = ((bf16[4,2,12288]{2,1,0:T(2,128)(2,1)}), bf16[4,2,12288]{2,1,0:T(2,128)(2,1)S(1)}, u32[]{:S(2)}, u32[]{:S(2)}) async-start(bf16[4,2,12288]{2,1,0:T(2,128)(2,1)} %reshape.122), calls=%async_computation.2 | async-start | bytes 393216 | tf_op jit(solution)/shard_map/all_to_all | solution.py:70
  40.5 7.5 %all-gather = bf16[16,2,4096]{2,1,0:T(2,128)(2,1)S(1)} all-gather(bf16[4,2,4096]{2,1,0:T(2,128)(2,1)S(1)} %all-to-all-done), channel_id=2, replica_groups=mesh['group'=2,'expert'=4,'dp'=4] {'dp'}, dimensions={0}, use_global_device_ids=true | all-gather | bytes 327680 | tf_op jit(solution)/shard_map/all_gather | solution.py:45
  48.0 0.1 reshape.109
  48.1 0.1 reshape.101
  48.2 0.0 copy-start.1
  48.2 2.2 %fusion.5 = f32[32,256]{1,0:T(8,128)S(1)} fusion(bf16[32,4096]{1,0:T(8,128)(2,1)S(1)} %reshape.101, bf16[1,4096,256]{2,1,0:T(8,128)(2,1)} %param.16), kind=kOutput, calls=%fused_computation.7 | convolution fusion | flops 67108864 | bytes 2392064 | tf_op jit(solution)/shard_map/dot_general | solution.py:82
  50.4 0.0 copy-done.1
  50.5 0.5 fusion.7
  50.9 0.0 all-to-all-done.2
  50.9 2.9 %reshape.123 = bf16[1024,1,6,16]{3,2,1,0:T(8,128)(2,1)} reshape(bf16[4,2,12288]{2,1,0:T(2,128)(2,1)S(1)} %all-to-all-done.2) | data formatting | bytes 393216
  53.9 2.5 %copy.48 = bf16[1,6,16,4,256]{4,3,2,1,0:T(4,128)(2,1)S(1)} copy(bf16[1,6,16,4,256]{2,1,4,3,0:T(8,128)(2,1)} %bitcast.50) | data formatting | bytes 393216 | tf_op jit(solution)/shard_map/all_to_all | solution.py:70
  56.4 0.0 all-gather.4.cloned.1.call-done
  56.4 4.2 %fusion.16 = bf16[32,16]{0,1:T(8,128)(2,1)S(1)} fusion(bf16[32,4096,1]{1,0,2:T(8,128)(2,1)S(1)} %reshape.109, bf16[1,24,16,4096]{3,2,0,1:T(8,128)(2,1)} %all-gather.4.cloned.1.call-done, f32[32,24]{0,1:T(8,128)S(1)} %fusion.27), kind=kOutput, calls=%fused_computation.14 | convolution fusion | flops 100687360 | bytes 3411968 | tf_op jit(solution)/shard_map/dot_general | solution.py:63
  60.7 0.2 fusion.20
  60.9 5.2 %all_gather.15 = bf16[32,1024]{1,0:T(8,128)(2,1)S(1)} all-gather(bf16[32,256]{1,0:T(8,128)(2,1)S(1)} %fusion.20), channel_id=1, replica_groups=mesh['group'=2,'expert'=4,'dp'=4] {'dp'}, dimensions={1}, use_global_device_ids=true | all-gather | bytes 81920 | tf_op jit(solution)/shard_map/all_gather | solution.py:87
  66.2 0.0 copy-done
  66.2 0.5 fusion.13
  66.6 0.7 reshape.102
  67.3 3.3 %all-to-all-start.3 = ((bf16[4,4,2,1024]{3,2,1,0:T(2,128)(2,1)}), bf16[4,4,2,1024]{3,2,1,0:T(2,128)(2,1)S(1)}, u32[]{:S(2)}, u32[]{:S(2)}) async-start(bf16[4,4,2,1024]{3,2,1,0:T(2,128)(2,1)} %reshape.102), calls=%async_computation.3 | async-start | bytes 131072 | tf_op jit(solution)/shard_map/all_to_all | solution.py:92
  70.6 0.1 select_reduce_fusion
  70.7 4.0 %all-to-all-done.3 = bf16[4,4,2,1024]{3,2,1,0:T(2,128)(2,1)S(1)} async-done(((bf16[4,4,2,1024]{3,2,1,0:T(2,128)(2,1)}), bf16[4,4,2,1024]{3,2,1,0:T(2,128)(2,1)S(1)}, u32[]{:S(2)}, u32[]{:S(2)}) %all-to-all-start.3) | async-done | bytes 65568 | tf_op jit(solution)/shard_map/all_to_all | solution.py:92
  74.7 0.7 copy.49
  75.4 5.1 %all-to-all-start.4 = ((bf16[1,4,2,4096]{3,2,0,1:T(2,128)(2,1)}), bf16[1,4,2,4096]{3,2,0,1:T(2,128)(2,1)S(1)}, u32[]{:S(2)}, u32[]{:S(2)}) async-start(bf16[1,4,2,4096]{3,2,0,1:T(2,128)(2,1)} %bitcast.16), calls=%async_computation.4 | async-start | bytes 131072 | tf_op jit(solution)/shard_map/all_to_all | solution.py:93
  80.5 5.7 %all-to-all-done.4 = bf16[1,4,2,4096]{3,2,0,1:T(2,128)(2,1)S(1)} async-done(((bf16[1,4,2,4096]{3,2,0,1:T(2,128)(2,1)}), bf16[1,4,2,4096]{3,2,0,1:T(2,128)(2,1)S(1)}, u32[]{:S(2)}, u32[]{:S(2)}) %all-to-all-start.4) | async-done | bytes 65568 | tf_op jit(solution)/shard_map/all_to_all | solution.py:93
  86.2 1.1 %fusion.9 = bf16[8,4096]{1,0:T(8,128)(2,1)} fusion(bf16[8,4096,1]{1,0,2:T(8,128)(2,1)S(1)} %reshape.110, f32[8,8]{1,0:T(8,128)S(1)} %get-tuple-element.5, s32[8,8]{1,0:T(8,128)S(1)} %multiply_add_fusion, pred[8,8]{1,0:T(8,128)(4,1)S(1)} %get-tuple-element.6), kind=kOutput, calls=%fused_computation.11 | convolution fusion | flops 4686848 | bytes 131648 | tf_op jit(solution)/shard_map/tkm,md->tkd/dot_general | solution.py:102
  (12 shorter events, 0.1 us)
Async XLA Ops:
  6.5 59.6 %copy-start = (bf16[1,1024,1024]{2,1,0:T(8,128)(2,1)S(1)}, bf16[1,1024,1024]{2,1,0:T(8,128)(2,1)}, u32[]{:S(2)}) copy-start(bf16[1,1024,1024]{2,1,0:T(8,128)(2,1)} %param.17) | copy-start | bytes 6291460
  6.5 49.9 %all-gather.4.cloned.1.call-start = ((), (), s32[]{:S(2)}) async-start(), calls=%async_computation.5 | async-start | bytes 3932160 | tf_op jit(solution)/shard_map/all_gather | solution.py:60
  9.8 15.6 %all-to-all-start.1 = ((s32[4,1,2]{2,1,0:T(1,128)}), s32[4,1,2]{2,1,0:T(1,128)S(1)}, u32[]{:S(2)}, u32[]{:S(2)}) async-start(s32[4,1,2]{2,1,0:T(1,128)} %copy.39), calls=%async_computation.1 | async-start | bytes 4096 | tf_op jit(solution)/shard_map/all_to_all | solution.py:42
  17.8 7.6 %copy-start.2 = (s32[8,8]{1,0:T(8,128)S(1)}, s32[8,8]{1,0:T(8,128)}, u32[]{:S(2)}) copy-start(s32[8,8]{1,0:T(8,128)} %param.11) | copy-start | bytes 772
  17.8 7.6 %copy-start.3 = (s32[8,8]{1,0:T(8,128)S(1)}, s32[8,8]{1,0:T(8,128)}, u32[]{:S(2)}) copy-start(s32[8,8]{1,0:T(8,128)} %param.12) | copy-start | bytes 772
  25.4 11.7 %all-to-all-start = ((bf16[4,2,4096]{2,1,0:T(2,128)(2,1)}), bf16[4,2,4096]{2,1,0:T(2,128)(2,1)S(1)}, u32[]{:S(2)}, u32[]{:S(2)}) async-start(bf16[4,2,4096]{2,1,0:T(2,128)(2,1)} %copy.38), calls=%async_computation | async-start | bytes 131072 | tf_op jit(solution)/shard_map/all_to_all | solution.py:41
  37.1 13.8 %all-to-all-start.2 = ((bf16[4,2,12288]{2,1,0:T(2,128)(2,1)}), bf16[4,2,12288]{2,1,0:T(2,128)(2,1)S(1)}, u32[]{:S(2)}, u32[]{:S(2)}) async-start(bf16[4,2,12288]{2,1,0:T(2,128)(2,1)} %reshape.122), calls=%async_computation.2 | async-start | bytes 393216 | tf_op jit(solution)/shard_map/all_to_all | solution.py:70
  48.2 2.2 %copy-start.1 = (bf16[1,4096,256]{2,1,0:T(8,128)(2,1)S(1)}, bf16[1,4096,256]{2,1,0:T(8,128)(2,1)}, u32[]{:S(2)}) copy-start(bf16[1,4096,256]{2,1,0:T(8,128)(2,1)} %param.15) | copy-start | bytes 6291460
  67.3 7.4 %all-to-all-start.3 = ((bf16[4,4,2,1024]{3,2,1,0:T(2,128)(2,1)}), bf16[4,4,2,1024]{3,2,1,0:T(2,128)(2,1)S(1)}, u32[]{:S(2)}, u32[]{:S(2)}) async-start(bf16[4,4,2,1024]{3,2,1,0:T(2,128)(2,1)} %reshape.102), calls=%async_computation.3 | async-start | bytes 131072 | tf_op jit(solution)/shard_map/all_to_all | solution.py:92
  75.4 10.8 %all-to-all-start.4 = ((bf16[1,4,2,4096]{3,2,0,1:T(2,128)(2,1)}), bf16[1,4,2,4096]{3,2,0,1:T(2,128)(2,1)S(1)}, u32[]{:S(2)}, u32[]{:S(2)}) async-start(bf16[1,4,2,4096]{3,2,0,1:T(2,128)(2,1)} %bitcast.16), calls=%async_computation.4 | async-start | bytes 131072 | tf_op jit(solution)/shard_map/all_to_all | solution.py:93
Sparse Core Ops, SparseCore 0:
  8.9 31.2 all-gather.3
where the time goes:
time: 95 us; the launch traced here: 94.2 us
  starting transfers between devices  23.2 us (24%)
  blocking collectives  18.1 us (19%)
  local copies, waits for them, and re-layouts  16.5 us (17%)
  between operations  13.5 us (14%)
  waiting for transfers between devices  10.5 us (11%)
  matrix products  9.7 us (10%)
  other arithmetic  2.62 us (3%)
    unnamed x11, local copies, waits for them, and re-layouts  9.81 us
    all_gather x1, blocking collectives, per_device(): lax.all_gather(got_rows[None], 'dp', axis=0, tiled=True)  7.51 us
    all_to_all x1, starting transfers between devices, per_device(): lax.all_to_all(send_ten, 'expert', split_axis=0, concat_axis=0, tiled=True)  6.35 us
    all_to_all x1, waiting for transfers between devices, per_device(): lax.all_to_all(home_rows, 'expert', split_axis=1, concat_axis=0, tiled=True)  5.74 us
    all_gather x1, blocking collectives, per_device(): lax.all_gather(got_ten[None], 'dp', axis=0, tiled=True)  5.35 us
    all_gather x1, blocking collectives, per_device(): lax.all_gather(hidden, 'dp', axis=1, tiled=True)  5.24 us
    all_to_all x1, starting transfers between devices, per_device(): lax.all_to_all(home_rows, 'expert', split_axis=1, concat_axis=0, tiled=True)  5.1 us
    all_to_all x1, starting transfers between devices, per_device(): lax.all_to_all(send_rows, 'expert', split_axis=0, concat_axis=0, tiled=True)  5.1 us
  transfers between devices with their start and end apart: 6, of which 2 were waited for; matrix products, arithmetic and copies ran while one was open for 23% of the time, Pallas kernels for 0%

commit v1 on v0

v1 whole, which is shorter than its diff:
```python
import functools

import jax
import jax.numpy as jnp
from jax import lax
from jax.experimental import pallas as pl
from jax.experimental.pallas import tpu as pltpu
from jax.sharding import PartitionSpec as P

MESH = pl.DeviceIdType.MESH
F32 = jnp.float32
BF16 = jnp.bfloat16


def iota(shape, dim):
    return lax.broadcasted_iota(jnp.int32, shape, dim)


def dot(a, b):
    return jnp.dot(a, b, preferred_element_type=F32)


def dot_nt(a, b):
    return lax.dot_general(a, b, (((1,), (1,)), ((), ())), preferred_element_type=F32)


def kernel(
    n_e,
    n_dp,
    tok,
    rout,
    gq,
    ten,
    look,
    gw,
    uw,
    dw,
    shr,
    exp,
    out,
    send,
    rows,
    spread,
    expand,
    hid,
    eout,
    back,
    gw_v,
    uw_v,
    dw_v,
    shr_v,
    load_sem,
    z_send,
    row_recv,
    f_send,
    x_send,
    x_recv,
    s_send,
    s_recv,
    h_send,
    h_recv,
    o_send,
    o_recv,
):
    e_me = lax.axis_index("expert")
    d_me = lax.axis_index("dp")
    tokens, width = tok.shape
    experts, tenants = look.shape
    topk = rout.shape[1]
    cap = send.shape[1]
    slots_out = experts * cap
    wide = send.shape[2]
    pages, rank_dim = shr_v.shape[:2]
    hidden_part = gw_v.shape[1]
    out_part = dw_v.shape[1]
    pr = pages * rank_dim

    barrier = pltpu.get_barrier_semaphore()
    for i in range(1, n_e):
        pl.semaphore_signal(
            barrier, inc=1, device_id={"expert": lax.rem(e_me + i, n_e)}, device_id_type=MESH
        )
    for i in range(1, n_dp):
        pl.semaphore_signal(
            barrier, inc=1, device_id={"dp": lax.rem(d_me + i, n_dp)}, device_id_type=MESH
        )

    loads = [
        pltpu.make_async_copy(shr.at[0], shr_v, load_sem.at[0]),
        pltpu.make_async_copy(gw.at[0], gw_v, load_sem.at[1]),
        pltpu.make_async_copy(uw.at[0], uw_v, load_sem.at[2]),
        pltpu.make_async_copy(
            exp.at[0, :, :, pl.ds(pl.multiple_of(d_me * hidden_part, hidden_part), hidden_part)],
            expand.at[d_me],
            load_sem.at[3],
        ),
        pltpu.make_async_copy(dw.at[0], dw_v, load_sem.at[4]),
    ]
    for c in loads:
        c.start()

    routing = rout[...]
    routing_f = routing.astype(F32)
    eye = (iota((topk, topk), 0) == iota((topk, topk), 1)).astype(F32)
    routing_t = dot_nt(eye, routing_f)
    j_row = iota((slots_out, tokens), 0)
    e_row = (j_row // cap).astype(F32)
    assign_t = jnp.zeros((slots_out, tokens), F32)
    for k in range(topk):
        assign_t += (routing_t[k : k + 1, :] == e_row).astype(F32)
    upper = (iota((tokens, tokens), 0) < iota((tokens, tokens), 1)).astype(F32)
    rank_t = dot(assign_t, upper)
    place_t = assign_t * (rank_t == lax.rem(j_row, cap).astype(F32)).astype(F32)
    x_out = dot(place_t.astype(BF16), tok[...])
    ten_row = iota((tokens, tenants), 0)
    ten_col = jnp.zeros((tokens, tenants), jnp.int32)
    for t in range(tokens):
        ten_col = jnp.where(ten_row == t, ten[t], ten_col)
    ten_hot = (ten_col == iota((tokens, tenants), 1)).astype(F32)
    slot_ten = dot(place_t, ten_hot)
    pick_e = (iota((slots_out, experts), 0) // cap == iota((slots_out, experts), 1)).astype(F32)
    look_rows = dot(pick_e, look[...].astype(F32))
    page = jnp.sum(slot_ten * look_rows, axis=1, keepdims=True)
    filled = jnp.sum(slot_ten, axis=1, keepdims=True)
    tail = wide - width
    page_hot = (page == iota((slots_out, tail), 1).astype(F32)).astype(F32) * filled
    for e in range(experts):
        send[e, :, :width] = x_out[e * cap : (e + 1) * cap, :].astype(BF16)
        send[e, :, width:] = page_hot[e * cap : (e + 1) * cap, :].astype(BF16)
    rows[e_me, d_me] = send[e_me]

    pl.semaphore_wait(barrier, n_e - 1 + n_dp - 1)

    waits = []
    order = sorted(range(1, n_e), key=lambda i: -min(i, n_e - i))
    for i in order:
        e = lax.rem(e_me + i, n_e)
        c = pltpu.make_async_remote_copy(
            src_ref=send.at[e],
            dst_ref=rows.at[e_me, d_me],
            send_sem=z_send.at[i],
            recv_sem=row_recv.at[e_me, d_me],
            device_id={"expert": e},
            device_id_type=MESH,
        )
        c.start()
        waits.append(c)

    def forward(z, slot):
        for i in range(1, n_dp):
            c = pltpu.make_async_remote_copy(
                src_ref=rows.at[z, d_me],
                dst_ref=rows.at[z, d_me],
                send_sem=f_send.at[slot, i],
                recv_sem=row_recv.at[z, d_me],
                device_id={"dp": lax.rem(d_me + i, n_dp)},
                device_id_type=MESH,
            )
            c.start()
            waits.append(c)

    def row_wait(z, d):
        pltpu.make_async_copy(rows.at[z, d], rows.at[z, d], row_recv.at[z, d]).wait()

    forward(e_me, 0)
    for i in range(1, n_dp):
        d = lax.rem(d_me + i, n_dp)
        c = pltpu.make_async_remote_copy(
            src_ref=exp.at[
                0, :, :, pl.ds(pl.multiple_of(d * hidden_part, hidden_part), hidden_part)
            ],
            dst_ref=expand.at[d_me],
            send_sem=x_send.at[i],
            recv_sem=x_recv.at[d_me],
            device_id={"dp": d},
            device_id_type=MESH,
        )
        c.start()
        waits.append(c)
    for i in sorted(range(1, n_e), key=lambda i: min(i, n_e - i)):
        z = lax.rem(e_me + i, n_e)
        row_wait(z, d_me)
        forward(z, i)
    for i in range(1, n_dp):
        for z in range(n_e):
            row_wait(z, lax.rem(d_me + i, n_dp))

    slot_count = n_e * n_dp * cap
    x_all = rows[...].astype(F32).reshape(slot_count, wide).astype(BF16)
    x_in = x_all[:, :width]
    hot = x_all[:, width:]
    loads[0].wait()
    products = dot_nt(x_in, shr_v[...].reshape(pr, width))
    own_pages = (
        iota((tail, pr), 0) == d_me * pages + iota((tail, pr), 1) // rank_dim
    ).astype(BF16)
    mask = dot(hot, own_pages)
    pad = spread.shape[2] - pr
    low = products.astype(BF16).astype(F32) * mask
    if pad:
        low = jnp.concatenate([low, jnp.zeros((slot_count, pad), F32)], axis=1)
    spread[d_me] = low.astype(BF16)
    for i in range(1, n_dp):
        c = pltpu.make_async_remote_copy(
            src_ref=spread.at[d_me],
            dst_ref=spread.at[d_me],
            send_sem=s_send.at[i],
            recv_sem=s_recv.at[d_me],
            device_id={"dp": lax.rem(d_me + i, n_dp)},
            device_id_type=MESH,
        )
        c.start()
        waits.append(c)

    loads[1].wait()
    gate_act = dot(x_in, gw_v[...])
    loads[2].wait()
    up_act = dot(x_in, uw_v[...])
    loads[3].wait()
    for i in range(n_dp):
        d = lax.rem(d_me + i, n_dp)
        if i:
            pltpu.make_async_copy(spread.at[d], spread.at[d], s_recv.at[d]).wait()
            pltpu.make_async_copy(expand.at[d], expand.at[d], x_recv.at[d]).wait()
        up_act += dot(spread[d][:, :pr], expand[d].reshape(pr, hidden_part))
    hidden = (gate_act / (1.0 + jnp.exp(-gate_act))) * up_act
    hid[d_me] = hidden.astype(BF16)
    for i in range(1, n_dp):
        c = pltpu.make_async_remote_copy(
            src_ref=hid.at[d_me],
            dst_ref=hid.at[d_me],
            send_sem=h_send.at[i],
            recv_sem=h_recv.at[d_me],
            device_id={"dp": lax.rem(d_me + i, n_dp)},
            device_id_type=MESH,
        )
        c.start()
        waits.append(c)

    j_col = iota((tokens, slots_out), 1)
    e_col = j_col // cap
    quant = gq[...]
    high = lax.shift_right_logical(quant, 8)
    rest = quant - high * 256
    assign = jnp.zeros((tokens, slots_out), F32)
    mix_high = jnp.zeros((tokens, slots_out), F32)
    mix_rest = jnp.zeros((tokens, slots_out), F32)
    for k in range(topk):
        hit = (routing[:, k : k + 1] == e_col).astype(F32)
        assign += hit
        mix_high += hit * (high[:, k : k + 1].astype(F32) * (256.0 / 32768.0))
        mix_rest += hit * (rest[:, k : k + 1].astype(F32) * (1.0 / 32768.0))
    lower = (iota((tokens, tokens), 1) < iota((tokens, tokens), 0)).astype(F32)
    rank = dot(lower, assign)
    here = (rank == lax.rem(j_col, cap).astype(F32)).astype(F32)
    mix = jnp.concatenate([mix_high * here, mix_rest * here], axis=0).astype(BF16)

    loads[4].wait()
    total = None
    for i in range(n_dp):
        d = lax.rem(d_me + i, n_dp)
        if i:
            pltpu.make_async_copy(hid.at[d], hid.at[d], h_recv.at[d]).wait()
        part = dot(
            hid[d], dw_v[pl.ds(pl.multiple_of(d * hidden_part, hidden_part), hidden_part), :]
        )
        total = part if total is None else total + part
    for z in range(n_e):
        for d in range(n_dp):
            base = (z * n_dp + d) * cap
            eout[z, d] = total[base : base + cap, :].astype(BF16)

    back[e_me, d_me] = eout[e_me, d_me]
    for i in sorted(range(n_e), key=lambda i: -min(i, n_e - i)):
        z = lax.rem(e_me + i, n_e)
        for j in range(n_dp - 1, -1, -1):
            if i == 0 and j == 0:
                continue
            d = lax.rem(d_me + j, n_dp)
            c = pltpu.make_async_remote_copy(
                src_ref=eout.at[z, d],
                dst_ref=back.at[e_me, d_me],
                send_sem=o_send.at[i, j],
                recv_sem=o_recv.at[e_me, d_me],
                device_id={"expert": z, "dp": d},
                device_id_type=MESH,
            )
            c.start()
            waits.append(c)
    for i in range(n_e):
        z = lax.rem(e_me + i, n_e)
        for j in range(n_dp):
            if i == 0 and j == 0:
                continue
            d = lax.rem(d_me + j, n_dp)
            pltpu.make_async_copy(back.at[z, d], back.at[z, d], o_recv.at[z, d]).wait()
    for d in range(n_dp):
        got = back[:, d].astype(F32).reshape(slots_out, out_part).astype(BF16)
        both = dot(mix, got)
        out[:, d * out_part : (d + 1) * out_part] = (both[:tokens] + both[tokens:]).astype(BF16)
    for c in waits:
        c.wait_send()


def per_device(n_e, n_dp, tok, rout, gq, ten, look, gw, uw, dw, shr, exp):
    tokens, width = tok.shape
    experts, tenants = look.shape
    cap = tokens // 4
    tail = -(-tenants // 128) * 128
    wide = width + tail
    pages, rank_dim = shr.shape[1:3]
    hidden_part = gw.shape[2]
    out_part = dw.shape[2]
    slot_count = n_e * n_dp * cap
    pr_pad = -(-pages * rank_dim // 128) * 128
    vmem = pl.BlockSpec(memory_space=pltpu.VMEM)
    hbm = pl.BlockSpec(memory_space=pl.ANY)
    dma = pltpu.SemaphoreType.DMA
    return pl.pallas_call(
        functools.partial(kernel, n_e, n_dp),
        out_shape=jax.ShapeDtypeStruct((tokens, width), BF16),
        in_specs=[
            vmem,
            vmem,
            vmem,
            pl.BlockSpec(memory_space=pltpu.SMEM),
            vmem,
            hbm,
            hbm,
            hbm,
            hbm,
            hbm,
        ],
        out_specs=vmem,
        scratch_shapes=[
            pltpu.VMEM((experts, cap, wide), BF16),
            pltpu.VMEM((n_e, n_dp, cap, wide), BF16),
            pltpu.VMEM((n_dp, slot_count, pr_pad), BF16),
            pltpu.VMEM((n_dp, pages, rank_dim, hidden_part), BF16),
            pltpu.VMEM((n_dp, slot_count, hidden_part), BF16),
            pltpu.VMEM((n_e, n_dp, cap, out_part), BF16),
            pltpu.VMEM((n_e, n_dp, cap, out_part), BF16),
            pltpu.VMEM(gw.shape[1:], BF16),
            pltpu.VMEM(uw.shape[1:], BF16),
            pltpu.VMEM(dw.shape[1:], BF16),
            pltpu.VMEM(shr.shape[1:], BF16),
            dma((5,)),
            dma((n_e,)),
            dma((n_e, n_dp)),
            dma((n_e, n_dp)),
            dma((n_dp,)),
            dma((n_dp,)),
            dma((n_dp,)),
            dma((n_dp,)),
            dma((n_dp,)),
            dma((n_dp,)),
            dma((n_e, n_dp)),
            dma((n_e, n_dp)),
        ],
        compiler_params=pltpu.CompilerParams(collective_id=0, has_side_effects=True),
    )(tok, rout, gq, ten, look, gw, uw, dw, shr, exp)


def solution(mesh):
    return jax.shard_map(
        functools.partial(per_device, mesh.shape["expert"], mesh.shape["dp"]),
        mesh=mesh,
        in_specs=(
            P(("group", "expert", "dp"), None),
            P(("group", "expert", "dp"), None),
            P(("group", "expert", "dp"), None),
            P(("group", "expert", "dp")),
            P(),
            P("expert", None, "dp"),
            P("expert", None, "dp"),
            P("expert", None, "dp"),
            P("expert", "dp", None, None),
            P("expert", "dp", None, None),
        ),
        out_specs=P(("group", "expert", "dp"), None),
        check_vma=False,
    )
```

time: 95 us -> 27.9 us (0.29)
  Pallas kernels: 0 us -> 26.3 us
  starting transfers between devices: 23.2 us -> 0 us
  blocking collectives: 18.1 us -> 0 us
  local copies, waits for them, and re-layouts: 16.5 us -> 1.47 us
  between operations: 13.5 us -> 0.01 us
  waiting for transfers between devices: 10.5 us -> 0 us
  matrix products: 9.7 us -> 0 us
  other arithmetic: 2.62 us -> 0 us
    pallas_call x0 -> x1, Pallas kernels: none -> 26.3 us  [per_device(): pl.pallas_call(functools.partial(kernel, n_e, n_dp), out_shape=jax.ShapeD...]
    all_to_all x5 -> x0, starting transfers between devices: 23.2 us -> none  [the longest x1 6.35 us: per_device(): lax.all_to_all(send_ten, 'expert', split_axis=0, concat_axis=0, tiled=True)]
    all_gather x3 -> x0, blocking collectives: 18.1 us -> none  [the longest x1 7.51 us: per_device(): lax.all_gather(got_rows[None], 'dp', axis=0, tiled=True)]
    all_to_all x5 -> x0, waiting for transfers between devices: 9.76 us -> none  [the longest x1 5.74 us: per_device(): lax.all_to_all(home_rows, 'expert', split_axis=1, concat_axis=0, tiled=True)]
    dot_general x7 -> x0, matrix products: 9.7 us -> none  [the longest x1 4.25 us: per_device(): lax.dot_general(slot_input, flat_pages, (((1,), (1,)), ((), ())), preferr...]
    unnamed x11 -> x1, local copies, waits for them, and re-layouts: 9.81 us -> 1.47 us
    all_to_all x4 -> x0, local copies, waits for them, and re-layouts: 3.85 us -> none  [the longest x2 2.5 us: per_device(): lax.all_to_all(adapter_expand, 'dp', split_axis=3, concat_axis=1, tiled=T...]
    reduce_sum x4 -> x0, other arithmetic: 1.14 us -> none  [the longest x1 0.83 us: slot_tables(): assign = jnp.sum(matches.astype(jnp.int32), axis=1)]
  transfers between devices with their start and end apart: 6 -> 0, of which waited for: 2 -> 0; matrix products, arithmetic and copies ran while one was open for 23% -> 0% of each run, Pallas kernels for 0% -> 0%
where the time goes in v1:
time: 27.9 us; the launch traced here: 27.7 us
  Pallas kernels  26.3 us (94%)
  local copies, waits for them, and re-layouts  1.47 us (5%)
    pallas_call x1, Pallas kernels, per_device(): pl.pallas_call(functools.partial(kernel, n_e, n_dp), out_shape=jax.ShapeD...  26.3 us
    unnamed x1, local copies, waits for them, and re-layouts  1.47 us

profile of v1, /device:TPU:0, one launch (start us, length us, event | category | flops | bytes accessed | tf_op | source)
XLA Modules:
  0.0 27.7 jit_solution(1170241306601100698)
XLA Ops:
  0.0 26.3 %shard_map.100 = bf16[8,4096]{1,0:T(8,128)(2,1)} custom-call(bf16[8,4096]{1,0:T(8,128)(2,1)} %tok.1, s32[8,8]{1,0:T(8,128)} %rout.1, s32[8,8]{1,0:T(8,128)} %gq.1, s32[8]{0:T(128)} %ten.1, s32[4,24]{1,0:T(4,128)} %look.1, bf16[1,4096,256]{2,1,0:T(8,128)(2,1)} %gw.1, bf16[1,4096,256]{2,1,0:T(8,128)(2,1)} %uw.1, bf16[1,1024,1024]{2,1,0:T(8,128)(2,1)} %dw.1, ...), custom_call_target="tpu_custom_call" | custom-call | tf_op jit(solution)/shard_map/pallas_call | solution.py:319
  26.3 1.5 %copy.12 = bf16[8,4096]{1,0:T(8,128)(2,1)} copy(bf16[8,4096]{1,0:T(8,128)(2,1)} %shard_map.100) | data formatting | bytes 131072

commit v2 on v1

--- a/solution.py
+++ b/solution.py
@@ -27,11 +27,11 @@
 def kernel(
     n_e,
     n_dp,
-    tok,
-    rout,
-    gq,
-    ten,
-    look,
+    tok_h,
+    rout_h,
+    gq_h,
+    ten_h,
+    look_h,
     gw,
     uw,
     dw,
@@ -49,6 +49,12 @@
     uw_v,
     dw_v,
     shr_v,
+    tok,
+    rout,
+    gq,
+    ten,
+    look,
+    small_sem,
     load_sem,
     z_send,
     row_recv,
@@ -85,6 +91,14 @@
             barrier, inc=1, device_id={"dp": lax.rem(d_me + i, n_dp)}, device_id_type=MESH
         )
 
+    small = [
+        pltpu.make_async_copy(src, dst, small_sem.at[i])
+        for i, (src, dst) in enumerate(
+            ((rout_h, rout), (ten_h, ten), (look_h, look), (tok_h, tok), (gq_h, gq))
+        )
+    ]
+    for c in small:
+        c.start()
     loads = [
         pltpu.make_async_copy(shr.at[0], shr_v, load_sem.at[0]),
         pltpu.make_async_copy(gw.at[0], gw_v, load_sem.at[1]),
@@ -99,6 +113,8 @@
     for c in loads:
         c.start()
 
+    for c in small:
+        c.wait()
     routing = rout[...]
     routing_f = routing.astype(F32)
     eye = (iota((topk, topk), 0) == iota((topk, topk), 1)).astype(F32)
@@ -318,19 +334,8 @@
     dma = pltpu.SemaphoreType.DMA
     return pl.pallas_call(
         functools.partial(kernel, n_e, n_dp),
-        out_shape=jax.ShapeDtypeStruct((tokens, width), BF16),
-        in_specs=[
-            vmem,
-            vmem,
-            vmem,
-            pl.BlockSpec(memory_space=pltpu.SMEM),
-            vmem,
-            hbm,
-            hbm,
-            hbm,
-            hbm,
-            hbm,
-        ],
+        out_shape=pltpu.VMEM((tokens, width), BF16),
+        in_specs=[hbm] * 10,
         out_specs=vmem,
         scratch_shapes=[
             pltpu.VMEM((experts, cap, wide), BF16),
@@ -344,6 +349,12 @@
             pltpu.VMEM(uw.shape[1:], BF16),
             pltpu.VMEM(dw.shape[1:], BF16),
             pltpu.VMEM(shr.shape[1:], BF16),
+            pltpu.VMEM(tok.shape, BF16),
+            pltpu.VMEM(rout.shape, jnp.int32),
+            pltpu.VMEM(gq.shape, jnp.int32),
+            pltpu.SMEM(ten.shape, jnp.int32),
+            pltpu.VMEM(look.shape, jnp.int32),
+            dma((5,)),
             dma((5,)),
             dma((n_e,)),
             dma((n_e, n_dp)),

time: 27.9 us -> 25.6 us (0.918)
  Pallas kernels: 26.3 us -> 24.8 us
  local copies, waits for them, and re-layouts: 1.47 us -> 0.63 us
    pallas_call x1, Pallas kernels: 26.3 us -> 24.8 us  [per_device(): pl.pallas_call(functools.partial(kernel, n_e, n_dp), out_shape=pltpu.VMEM...]
    unnamed x1, local copies, waits for them, and re-layouts: 1.47 us -> 0.63 us
where the time goes in v2:
time: 25.6 us; the launch traced here: 25.5 us
  Pallas kernels  24.8 us (97%)
  local copies, waits for them, and re-layouts  0.63 us (2%)
    pallas_call x1, Pallas kernels, per_device(): pl.pallas_call(functools.partial(kernel, n_e, n_dp), out_shape=pltpu.VMEM...  24.8 us
    unnamed x1, local copies, waits for them, and re-layouts  0.63 us

profile of v2, /device:TPU:0, one launch (start us, length us, event | category | flops | bytes accessed | tf_op | source)
XLA Modules:
  0.0 25.5 jit_solution(14084657140876009371)
XLA Ops:
  0.0 24.8 %shard_map.100 = bf16[8,4096]{1,0:T(8,128)(2,1)S(1)} custom-call(bf16[8,4096]{1,0:T(8,128)(2,1)} %tok_h.1, s32[8,8]{1,0:T(8,128)} %rout_h.1, s32[8,8]{1,0:T(8,128)} %gq_h.1, s32[8]{0:T(128)} %ten_h.1, s32[4,24]{1,0:T(4,128)} %look_h.1, bf16[1,4096,256]{2,1,0:T(8,128)(2,1)} %gw.1, bf16[1,4096,256]{2,1,0:T(8,128)(2,1)} %uw.1, bf16[1,1024,1024]{2,1,0:T(8,128)(2,1)} %dw.1, ...), custom_call_target="tpu_custom_call" | custom-call | tf_op jit(solution)/shard_map/pallas_call | solution.py:335
  24.8 0.6 %copy.12 = bf16[8,4096]{1,0:T(8,128)(2,1)} copy(bf16[8,4096]{1,0:T(8,128)(2,1)S(1)} %shard_map.100) | data formatting | bytes 131072

commit v3 on v2

--- a/solution.py
+++ b/solution.py
@@ -14,6 +14,17 @@
 
 def iota(shape, dim):
     return lax.broadcasted_iota(jnp.int32, shape, dim)
+
+
+def near(e, k, n):
+    low = jnp.minimum(e, n - 1 - e)
+    pair = e - (k + 1) // 2 if k % 2 else e + k // 2
+    rest = jnp.where(2 * e < n - 1, k, n - 1 - k)
+    return jnp.where(k <= 2 * low, pair, rest)
+
+
+def far_first(n):
+    return sorted(range(1, n), key=lambda i: abs(i - n // 2))
 
 
 def dot(a, b):
@@ -287,8 +298,8 @@
             eout[z, d] = total[base : base + cap, :].astype(BF16)
 
     back[e_me, d_me] = eout[e_me, d_me]
-    for i in sorted(range(n_e), key=lambda i: -min(i, n_e - i)):
-        z = lax.rem(e_me + i, n_e)
+    for i in range(n_e - 1, -1, -1):
+        z = near(e_me, i, n_e)
         for j in range(n_dp - 1, -1, -1):
             if i == 0 and j == 0:
                 continue

time: 25.6 us -> 25.4 us (level)
  no operation moved by 1% of the time
where the time goes in v3:
time: 25.4 us; the launch traced here: 25.2 us
  Pallas kernels  24.6 us (97%)
  local copies, waits for them, and re-layouts  0.63 us (2%)
    pallas_call x1, Pallas kernels, per_device(): pl.pallas_call(functools.partial(kernel, n_e, n_dp), out_shape=pltpu.VMEM...  24.6 us
    unnamed x1, local copies, waits for them, and re-layouts  0.63 us

profile of v3, /device:TPU:0, one launch (start us, length us, event | category | flops | bytes accessed | tf_op | source)
XLA Modules:
  0.0 25.2 jit_solution(16299581096860985539)
XLA Ops:
  0.0 24.6 %shard_map.100 = bf16[8,4096]{1,0:T(8,128)(2,1)S(1)} custom-call(bf16[8,4096]{1,0:T(8,128)(2,1)} %tok_h.1, s32[8,8]{1,0:T(8,128)} %rout_h.1, s32[8,8]{1,0:T(8,128)} %gq_h.1, s32[8]{0:T(128)} %ten_h.1, s32[4,24]{1,0:T(4,128)} %look_h.1, bf16[1,4096,256]{2,1,0:T(8,128)(2,1)} %gw.1, bf16[1,4096,256]{2,1,0:T(8,128)(2,1)} %uw.1, bf16[1,1024,1024]{2,1,0:T(8,128)(2,1)} %dw.1, ...), custom_call_target="tpu_custom_call" | custom-call | tf_op jit(solution)/shard_map/pallas_call | solution.py:346
  24.6 0.6 %copy.12 = bf16[8,4096]{1,0:T(8,128)(2,1)} copy(bf16[8,4096]{1,0:T(8,128)(2,1)S(1)} %shard_map.100) | data formatting | bytes 131072
